TPU v7x, 32 devices: a whole 2x2x4 slice. The times are simulated.
32 devices in a mesh: space: 16 (over z, y, x), src: 2 (over core).
Axes of the slice: x: 2, y: 2, z: 4, core: 2. Of those that a mesh axis runs over, the one named last changes fastest.
Arguments:
- rhs: float32 [12288, 1024], P('space', 'src'), may hold values from -18 to 18
- diag_blocks: bfloat16 [48, 256, 256], P('space', 'src'), may hold values from -0.5 to 5.5
- couple_blocks: bfloat16 [48, 2, 256, 256], P('space', None, 'src'), may hold values from -0.1875 to 0.1875
- halo_weight: bfloat16 [32, 256, 128], P('space', 'src'), may hold values from -0.25 to 0.25
- neighbours: int32 [48, 2], P('space'), may hold values from 0 to 2
- boundary: int32 [32, 128], P('space'), may hold values from 0 to 767
Outputs:
- solution: float32 [12288, 1024], P('space', 'src')
- misfit: float32 [1024], P('src')
All inputs are finite; a program needn't handle non-finite values.
Results may differ from a plain program's by a relative error of at most 0.0032.
Values may be sent and summed in bfloat16 or wider, within the bound.
A program may use at most 64 MiB of HBM per device.

v0:
```python
import jax
import jax.numpy as jnp
from jax import lax
from jax.sharding import PartitionSpec as P

SWEEPS = 4


centre = 4.0
half_width = 2.0


def passed_along(x, axis, by):
    size = lax.axis_size(axis)
    pairs = [(i, i + by) for i in range(size) if 0 <= i + by < size]
    return lax.ppermute(x, axis, pairs)


def apply_operator(direction, blocks, neighbours, boundary):
    diag_full, couple_full, halo_full = blocks
    edges = direction.shape[0]
    width = direction.shape[1]
    agg_count = diag_full.shape[0]
    block_size = diag_full.shape[1]
    flat_rounded = direction.astype(jnp.bfloat16)
    send_up = jnp.take(flat_rounded, boundary[1], axis=0)
    send_down = jnp.take(flat_rounded, boundary[0], axis=0)
    from_below = passed_along(send_up, "space", 1)
    from_above = passed_along(send_down, "space", -1)
    rounded = flat_rounded.reshape(agg_count, block_size, width)
    self_term = jnp.einsum("aij,ajs->ais", diag_full, rounded, preferred_element_type=jnp.float32)
    beside = rounded[neighbours]
    cross_term = jnp.einsum(
        "akij,akjs->ais", couple_full, beside, preferred_element_type=jnp.float32
    )
    lower = jnp.dot(halo_full[0], from_below, preferred_element_type=jnp.float32)
    upper = jnp.dot(halo_full[1], from_above, preferred_element_type=jnp.float32)
    total = self_term + cross_term
    total = total.at[0].add(lower)
    total = total.at[agg_count - 1].add(upper)
    return total.reshape(edges, width)


def local(rhs, diag_blocks, couple_blocks, halo_weight, neighbours, boundary):
    resident = (
        lax.all_gather(diag_blocks, "src", axis=1, tiled=True),
        lax.all_gather(couple_blocks, "src", axis=2, tiled=True),
        lax.all_gather(halo_weight, "src", axis=1, tiled=True),
    )
    rhs_part = jnp.sum(rhs * rhs, axis=0)
    rhs_total = lax.psum(rhs_part, "space")
    residual = rhs
    solution = jnp.zeros_like(rhs)
    direction = rhs / centre
    sigma = centre / half_width
    ratio = 1.0 / sigma
    for sweep in range(SWEEPS):
        solution = solution + direction
        residual = residual - apply_operator(direction, resident, neighbours, boundary)
        if sweep + 1 < SWEEPS:
            ratio_new = 1.0 / (2.0 * sigma - ratio)
            direction = ratio_new * ratio * direction + 2.0 * ratio_new / half_width * residual
            ratio = ratio_new
    res_part = jnp.sum(residual * residual, axis=0)
    res_total = lax.psum(res_part, "space")
    misfit = jnp.sqrt(res_total / (rhs_total + 1e-06))
    return (solution, misfit)


def solution(mesh):
    placed = (
        P("space", "src"),
        P("space", "src", None),
        P("space", None, "src", None),
        P("space", "src", None),
        P("space", None),
        P("space", None),
    )
    return jax.shard_map(
        local, mesh=mesh, in_specs=placed, out_specs=(P("space", "src"), P("src")), check_vma=False
    )
```

profile of v0, /device:TPU:0, one launch (start us, length us, event | category | flops | bytes accessed | tf_op | source)
XLA Modules:
  0.0 126.7 jit_solution(17712593504281664859)
XLA Ops:
  0.6 1.6 %multiply_convert_fusion = bf16[768,512]{1,0:T(8,128)(2,1)S(1)} fusion(f32[768,512]{1,0:T(8,128)} %param.24), kind=kLoop, calls=%fused_computation.31 | loop fusion | flops 786432 | bytes 2359296 | tf_op jit(solution)/shard_map/convert_element_type | solution.py:25
  2.3 0.8 gather_fusion.4
  3.2 0.7 broadcast_select_fusion.7
  3.9 5.5 %collective-permute-start = (bf16[128,512]{1,0:T(8,128)(2,1)}, bf16[128,512]{1,0:T(8,128)(2,1)}, u32[]{:S(2)}, u32[]{:S(2)}) collective-permute-start(bf16[128,512]{1,0:T(8,128)(2,1)} %broadcast_select_fusion.7), channel_id=1, source_target_pairs={{0,2},{2,4},{4,6},{6,8},{8,10},{10,12},{12,14},{14,16},{16,18},{18... | collective-permute-start | bytes 393224 | tf_op jit(solution)/shard_map/ppermute | solution.py:16
  9.4 0.8 gather_fusion.5
  10.3 0.7 broadcast_select_fusion.3
  11.0 1.3 %collective-permute-start.1 = (bf16[128,512]{1,0:T(8,128)(2,1)}, bf16[128,512]{1,0:T(8,128)(2,1)}, u32[]{:S(2)}, u32[]{:S(2)}) collective-permute-start(bf16[128,512]{1,0:T(8,128)(2,1)} %broadcast_select_fusion.3), channel_id=1, source_target_pairs={{2,0},{4,2},{6,4},{8,6},{10,8},{12,10},{14,12},{16,14},{18,16},{20... | collective-permute-start | bytes 393224 | tf_op jit(solution)/shard_map/ppermute | solution.py:16
  12.3 2.4 %all_gather.10 = bf16[3,2,256,256]{3,2,1,0:T(8,128)(2,1)S(1)} all-gather(bf16[3,2,128,256]{3,2,1,0:T(8,128)(2,1)S(1)} %copy-done.17), channel_id=1, replica_groups=mesh['space'=16,'src'=2] {'src'}, dimensions={2}, use_global_device_ids=true | all-gather | bytes 1179648 | tf_op jit(solution)/shard_map/all_gather | solution.py:47
  14.9 2.1 %all_gather.9 = bf16[3,256,256]{2,1,0:T(8,128)(2,1)S(1)} all-gather(bf16[3,128,256]{2,1,0:T(8,128)(2,1)S(1)} %copy-done.18), channel_id=1, replica_groups=mesh['space'=16,'src'=2] {'src'}, dimensions={1}, use_global_device_ids=true | all-gather | bytes 589824 | tf_op jit(solution)/shard_map/all_gather | solution.py:46
  17.0 0.6 gather_fusion
  17.6 0.6 fusion.22
  18.6 0.5 copy-done.19
  19.0 2.0 %all_gather.11 = bf16[2,256,128]{2,1,0:T(8,128)(2,1)S(1)} all-gather(bf16[2,128,128]{2,1,0:T(8,128)(2,1)S(1)} %copy-done.19), channel_id=1, replica_groups=mesh['space'=16,'src'=2] {'src'}, dimensions={1}, use_global_device_ids=true | all-gather | bytes 196608 | tf_op jit(solution)/shard_map/all_gather | solution.py:48
  21.1 1.2 fusion.7
  22.3 1.1 fusion.18
  23.4 0.4 fusion.21
  23.8 1.5 %gather_fusion.6 = bf16[128,512]{1,0:T(8,128)(2,1)} fusion(bf16[768,512]{1,0:T(8,128)(2,1)S(1)} %fusion.21, s32[1024]{0:T(1024)S(1)} %pad_clamp_fusion.1), kind=kCustom, calls=%fused_computation.2.clone | custom fusion | bytes 262656 | tf_op jit(solution)/shard_map/jit(_take)/gather | solution.py:26
  25.3 1.6 %gather_fusion.7 = bf16[128,512]{1,0:T(8,128)(2,1)} fusion(bf16[768,512]{1,0:T(8,128)(2,1)S(1)} %fusion.21, s32[1024]{0:T(1024)} %copy-done.20), kind=kCustom, calls=%fused_computation.3.clone | custom fusion | bytes 262656 | tf_op jit(solution)/shard_map/jit(_take)/gather | solution.py:27
  26.9 1.8 %gather_fusion.1 = bf16[6,256,512]{2,1,0:T(8,128)(2,1)} fusion(bf16[3,256,512]{2,1,0:T(8,128)(2,1)S(1)} %bitcast.180, s32[1024]{0:T(1024)S(1)} %pad_clamp_fusion.2), kind=kCustom, calls=%fused_computation.9 | custom fusion | bytes 3145752 | tf_op jit(solution)/shard_map/gather | solution.py:32
  28.8 2.0 %fusion.23 = f32[3,512,256,1]{1,2,3,0:T(8,128)S(1)} fusion(bf16[3,2,256,256]{3,2,1,0:T(8,128)(2,1)S(1)} %all_gather.10, bf16[3,2,256,512]{3,2,1,0:T(8,128)(2,1)} %bitcast.184), kind=kOutput, calls=%fused_computation.80 | convolution fusion | flops 402653184 | bytes 3932160 | tf_op jit(solution)/shard_map/akij,akjs->ais/dot_general | solution.py:33
  31.2 0.5 copy-done.15
  31.8 4.7 %collective-permute-start.2 = (bf16[128,512]{1,0:T(8,128)(2,1)S(1)}, bf16[128,512]{1,0:T(8,128)(2,1)S(1)}, u32[]{:S(2)}, u32[]{:S(2)}) collective-permute-start(bf16[128,512]{1,0:T(8,128)(2,1)S(1)} %broadcast_select_fusion.6), channel_id=1, source_target_pairs={{0,2},{2,4},{4,6},{6,8},{8,10},{10,12},{12,14},{14,16},{16,18},{18... | collective-permute-start | bytes 393224 | tf_op jit(solution)/shard_map/ppermute | solution.py:16
  36.6 1.3 %collective-permute-start.3 = (bf16[128,512]{1,0:T(8,128)(2,1)S(1)}, bf16[128,512]{1,0:T(8,128)(2,1)S(1)}, u32[]{:S(2)}, u32[]{:S(2)}) collective-permute-start(bf16[128,512]{1,0:T(8,128)(2,1)S(1)} %broadcast_select_fusion.2), channel_id=1, source_target_pairs={{2,0},{4,2},{6,4},{8,6},{10,8},{12,10},{14,12},{16,14},{18,16},{20... | collective-permute-start | bytes 393224 | tf_op jit(solution)/shard_map/ppermute | solution.py:16
  37.9 1.7 %collective-permute-done.2 = bf16[128,512]{1,0:T(8,128)(2,1)S(1)} collective-permute-done((bf16[128,512]{1,0:T(8,128)(2,1)S(1)}, bf16[128,512]{1,0:T(8,128)(2,1)S(1)}, u32[]{:S(2)}, u32[]{:S(2)}) %collective-permute-start.2) | collective-permute-done | bytes 131104 | tf_op jit(solution)/shard_map/ppermute | solution.py:16
  39.8 4.8 %collective-permute-done.3 = bf16[128,512]{1,0:T(8,128)(2,1)S(1)} collective-permute-done((bf16[128,512]{1,0:T(8,128)(2,1)S(1)}, bf16[128,512]{1,0:T(8,128)(2,1)S(1)}, u32[]{:S(2)}, u32[]{:S(2)}) %collective-permute-start.3) | collective-permute-done | bytes 131104 | tf_op jit(solution)/shard_map/ppermute | solution.py:16
  44.8 2.4 %fusion.19 = (bf16[768,512]{1,0:T(8,128)(2,1)S(1)}, f32[768,512]{1,0:T(8,128)}, f32[512]{0:T(512)}) fusion(f32[768,512]{1,0:T(8,128)S(1)} %copy-done.1, f32[3,256,512]{2,1,0:T(8,128)S(1)} %fusion.18, f32[3,256,512]{2,1,0:T(8,128)S(1)} %fusion.17), kind=kLoop, calls=%fused_computation.57 | loop fusion | flops 4324864 | bytes 7079936 | tf_op jit(solution)/shard_map/convert_element_type | solution.py:25
  47.2 1.5 %gather_fusion.8 = bf16[128,512]{1,0:T(8,128)(2,1)} fusion(bf16[768,512]{1,0:T(8,128)(2,1)S(1)} %get-tuple-element.101, s32[1024]{0:T(1024)S(1)} %pad_clamp_fusion.1), kind=kCustom, calls=%fused_computation.4.clone | custom fusion | bytes 262656 | tf_op jit(solution)/shard_map/jit(_take)/gather | solution.py:26
  48.7 1.6 %gather_fusion.9 = bf16[128,512]{1,0:T(8,128)(2,1)} fusion(bf16[768,512]{1,0:T(8,128)(2,1)S(1)} %get-tuple-element.101, s32[1024]{0:T(1024)} %copy-done.20), kind=kCustom, calls=%fused_computation.5.clone | custom fusion | bytes 262656 | tf_op jit(solution)/shard_map/jit(_take)/gather | solution.py:27
  50.3 1.8 %gather_fusion.2 = bf16[6,256,512]{2,1,0:T(8,128)(2,1)} fusion(bf16[3,256,512]{2,1,0:T(8,128)(2,1)S(1)} %bitcast.178, s32[1024]{0:T(1024)S(1)} %pad_clamp_fusion.2), kind=kCustom, calls=%fused_computation.10 | custom fusion | bytes 3145752 | tf_op jit(solution)/shard_map/gather | solution.py:32
  52.1 2.0 %fusion.24 = f32[3,512,256,1]{1,2,3,0:T(8,128)S(1)} fusion(bf16[3,2,256,256]{3,2,1,0:T(8,128)(2,1)S(1)} %all_gather.10, bf16[3,2,256,512]{3,2,1,0:T(8,128)(2,1)} %bitcast.185), kind=kOutput, calls=%fused_computation.81 | convolution fusion | flops 402653184 | bytes 3932160 | tf_op jit(solution)/shard_map/akij,akjs->ais/dot_general | solution.py:33
  54.5 0.5 copy-done.16
  55.1 3.9 %collective-permute-start.4 = (bf16[128,512]{1,0:T(8,128)(2,1)S(1)}, bf16[128,512]{1,0:T(8,128)(2,1)S(1)}, u32[]{:S(2)}, u32[]{:S(2)}) collective-permute-start(bf16[128,512]{1,0:T(8,128)(2,1)S(1)} %broadcast_select_fusion.5), channel_id=1, source_target_pairs={{0,2},{2,4},{4,6},{6,8},{8,10},{10,12},{12,14},{14,16},{16,18},{18... | collective-permute-start | bytes 393224 | tf_op jit(solution)/shard_map/ppermute | solution.py:16
  59.1 1.3 %collective-permute-start.5 = (bf16[128,512]{1,0:T(8,128)(2,1)S(1)}, bf16[128,512]{1,0:T(8,128)(2,1)S(1)}, u32[]{:S(2)}, u32[]{:S(2)}) collective-permute-start(bf16[128,512]{1,0:T(8,128)(2,1)S(1)} %broadcast_select_fusion.1), channel_id=1, source_target_pairs={{2,0},{4,2},{6,4},{8,6},{10,8},{12,10},{14,12},{16,14},{18,16},{20... | collective-permute-start | bytes 393224 | tf_op jit(solution)/shard_map/ppermute | solution.py:16
  60.4 1.1 collective-permute-done.4
  61.7 4.3 %collective-permute-done.5 = bf16[128,512]{1,0:T(8,128)(2,1)S(1)} collective-permute-done((bf16[128,512]{1,0:T(8,128)(2,1)S(1)}, bf16[128,512]{1,0:T(8,128)(2,1)S(1)}, u32[]{:S(2)}, u32[]{:S(2)}) %collective-permute-start.5) | collective-permute-done | bytes 131104 | tf_op jit(solution)/shard_map/ppermute | solution.py:16
  66.2 2.0 %fusion.14 = (bf16[768,512]{1,0:T(8,128)(2,1)S(1)}, f32[768,512]{1,0:T(8,128)}) fusion(f32[768,512]{1,0:T(8,128)S(1)} %copy-done.5, f32[3,256,512]{2,1,0:T(8,128)S(1)} %fusion.16, f32[768,512]{1,0:T(8,128)S(1)} %copy-done.2, f32[3,256,512]{2,1,0:T(8,128)S(1)} %fusion.18), kind=kLoop, calls=%fused_computation.48 | loop fusion | flops 6291456 | bytes 8650752 | tf_op jit(solution)/shard_map/convert_element_type | solution.py:25
  68.3 1.5 %gather_fusion.10 = bf16[128,512]{1,0:T(8,128)(2,1)} fusion(bf16[768,512]{1,0:T(8,128)(2,1)S(1)} %get-tuple-element.107, s32[1024]{0:T(1024)S(1)} %pad_clamp_fusion.1), kind=kCustom, calls=%fused_computation.6.clone | custom fusion | bytes 262656 | tf_op jit(solution)/shard_map/jit(_take)/gather | solution.py:26
  69.8 1.6 %gather_fusion.11 = bf16[128,512]{1,0:T(8,128)(2,1)} fusion(bf16[768,512]{1,0:T(8,128)(2,1)S(1)} %get-tuple-element.107, s32[1024]{0:T(1024)} %copy-done.20), kind=kCustom, calls=%fused_computation.7.clone | custom fusion | bytes 262656 | tf_op jit(solution)/shard_map/jit(_take)/gather | solution.py:27
  71.4 0.6 gather_fusion.3
  72.0 0.6 fusion.25
  73.0 0.5 copy-done.12
  73.6 5.6 %collective-permute-start.6 = (bf16[128,512]{1,0:T(8,128)(2,1)S(1)}, bf16[128,512]{1,0:T(8,128)(2,1)S(1)}, u32[]{:S(2)}, u32[]{:S(2)}) collective-permute-start(bf16[128,512]{1,0:T(8,128)(2,1)S(1)} %broadcast_select_fusion.4), channel_id=1, source_target_pairs={{0,2},{2,4},{4,6},{6,8},{8,10},{10,12},{12,14},{14,16},{16,18},{18... | collective-permute-start | bytes 393224 | tf_op jit(solution)/shard_map/ppermute | solution.py:16
  79.3 1.3 %collective-permute-start.7 = (bf16[128,512]{1,0:T(8,128)(2,1)S(1)}, bf16[128,512]{1,0:T(8,128)(2,1)S(1)}, u32[]{:S(2)}, u32[]{:S(2)}) collective-permute-start(bf16[128,512]{1,0:T(8,128)(2,1)S(1)} %broadcast_select_fusion), channel_id=1, source_target_pairs={{2,0},{4,2},{6,4},{8,6},{10,8},{12,10},{14,12},{16,14},{18,16},{20... | collective-permute-start | bytes 393224 | tf_op jit(solution)/shard_map/ppermute | solution.py:16
  80.6 1.1 collective-permute-done.6
  81.9 4.2 %collective-permute-done.7 = bf16[128,512]{1,0:T(8,128)(2,1)S(1)} collective-permute-done((bf16[128,512]{1,0:T(8,128)(2,1)S(1)}, bf16[128,512]{1,0:T(8,128)(2,1)S(1)}, u32[]{:S(2)}, u32[]{:S(2)}) %collective-permute-start.7) | collective-permute-done | bytes 131104 | tf_op jit(solution)/shard_map/ppermute | solution.py:16
  86.4 0.4 fusion.1
  87.1 39.1 %all-reduce = (f32[512]{0:T(512)S(1)}, f32[512]{0:T(512)S(1)}) all-reduce(f32[512]{0:T(512)S(1)} %fusion.1, f32[512]{0:T(512)S(1)} %copy-done.21), channel_id=1, replica_groups=mesh['space'=16,'src'=2] {'space'}, use_global_device_ids=true, to_apply=%region_1.3 | all-reduce | flops 1024 | bytes 8192 | tf_op jit(solution)/shard_map/psum | solution.py:65
  126.1 0.6 fusion.20
  (69 shorter events, 3.9 us)
Async XLA Ops:
  0.6 1.6 %copy-start.22 = (s32[2,128]{1,0:T(2,128)S(1)}, s32[2,128]{1,0:T(2,128)}, u32[]{:S(2)}) copy-start(s32[2,128]{1,0:T(2,128)} %param.29) | copy-start | bytes 3076
  2.3 10.1 %copy-start.17 = (bf16[3,2,128,256]{3,2,1,0:T(8,128)(2,1)S(1)}, bf16[3,2,128,256]{3,2,1,0:T(8,128)(2,1)}, u32[]{:S(2)}) copy-start(bf16[3,2,128,256]{3,2,1,0:T(8,128)(2,1)} %param.26) | copy-start | bytes 1179652
  3.2 11.5 %copy-start.23 = (s32[3,2]{0,1:T(2,128)S(1)}, s32[3,2]{0,1:T(2,128)}, u32[]{:S(2)}) copy-start(s32[3,2]{0,1:T(2,128)} %param.28) | copy-start | bytes 76
  3.2 11.7 %copy-start.18 = (bf16[3,128,256]{2,1,0:T(8,128)(2,1)S(1)}, bf16[3,128,256]{2,1,0:T(8,128)(2,1)}, u32[]{:S(2)}) copy-start(bf16[3,128,256]{2,1,0:T(8,128)(2,1)} %param.25) | copy-start | bytes 589828
  3.9 17.2 %collective-permute-start = (bf16[128,512]{1,0:T(8,128)(2,1)}, bf16[128,512]{1,0:T(8,128)(2,1)}, u32[]{:S(2)}, u32[]{:S(2)}) collective-permute-start(bf16[128,512]{1,0:T(8,128)(2,1)} %broadcast_select_fusion.7), channel_id=1, source_target_pairs={{0,2},{2,4},{4,6},{6,8},{8,10},{10,12},{12,14},{14,16},{16,18},{18... | collective-permute-start | bytes 393224 | tf_op jit(solution)/shard_map/ppermute | solution.py:16
  9.4 5.4 %copy-start.20 = (s32[1024]{0:T(1024)}, s32[1024]{0:T(1024)S(1)}, u32[]{:S(2)}) copy-start(s32[1024]{0:T(1024)S(1)} %pad_clamp_fusion) | copy-start | bytes 12292
  11.0 11.2 %collective-permute-start.1 = (bf16[128,512]{1,0:T(8,128)(2,1)}, bf16[128,512]{1,0:T(8,128)(2,1)}, u32[]{:S(2)}, u32[]{:S(2)}) collective-permute-start(bf16[128,512]{1,0:T(8,128)(2,1)} %broadcast_select_fusion.3), channel_id=1, source_target_pairs={{2,0},{4,2},{6,4},{8,6},{10,8},{12,10},{14,12},{16,14},{18,16},{20... | collective-permute-start | bytes 393224 | tf_op jit(solution)/shard_map/ppermute | solution.py:16
  18.2 0.8 copy-start.19
  19.0 4.4 %copy-start = (f32[768,512]{1,0:T(8,128)S(1)}, f32[768,512]{1,0:T(8,128)}, u32[]{:S(2)}) copy-start(f32[768,512]{1,0:T(8,128)} %param.24) | copy-start | bytes 4718596
  21.1 1.2 copy-start.7
  30.8 0.9 copy-start.15
  30.8 5.7 %copy-start.13 = (bf16[128,512]{1,0:T(8,128)(2,1)S(1)}, bf16[128,512]{1,0:T(8,128)(2,1)}, u32[]{:S(2)}) copy-start(bf16[128,512]{1,0:T(8,128)(2,1)} %gather_fusion.7) | copy-start | bytes 393220
  30.8 8.7 %copy-start.8 = (bf16[2,256,128]{2,1,0:T(8,128)(2,1)S(1)}, bf16[2,256,128]{2,1,0:T(8,128)(2,1)}, u32[]{:S(2)}) copy-start(bf16[2,256,128]{2,1,0:T(8,128)(2,1)} %copy-done.7) | copy-start | bytes 393220
  31.7 13.1 %copy-start.1 = (f32[768,512]{1,0:T(8,128)S(1)}, f32[768,512]{1,0:T(8,128)}, u32[]{:S(2)}) copy-start(f32[768,512]{1,0:T(8,128)} %param.24) | copy-start | bytes 4718596
  31.8 7.8 %collective-permute-start.2 = (bf16[128,512]{1,0:T(8,128)(2,1)S(1)}, bf16[128,512]{1,0:T(8,128)(2,1)S(1)}, u32[]{:S(2)}, u32[]{:S(2)}) collective-permute-start(bf16[128,512]{1,0:T(8,128)(2,1)S(1)} %broadcast_select_fusion.6), channel_id=1, source_target_pairs={{0,2},{2,4},{4,6},{6,8},{8,10},{10,12},{12,14},{14,16},{16,18},{18... | collective-permute-start | bytes 393224 | tf_op jit(solution)/shard_map/ppermute | solution.py:16
  36.6 8.0 %collective-permute-start.3 = (bf16[128,512]{1,0:T(8,128)(2,1)S(1)}, bf16[128,512]{1,0:T(8,128)(2,1)S(1)}, u32[]{:S(2)}, u32[]{:S(2)}) collective-permute-start(bf16[128,512]{1,0:T(8,128)(2,1)S(1)} %broadcast_select_fusion.2), channel_id=1, source_target_pairs={{2,0},{4,2},{6,4},{8,6},{10,8},{12,10},{14,12},{16,14},{18,16},{20... | collective-permute-start | bytes 393224 | tf_op jit(solution)/shard_map/ppermute | solution.py:16
  54.1 0.9 copy-start.16
  54.1 4.9 %copy-start.14 = (bf16[128,512]{1,0:T(8,128)(2,1)S(1)}, bf16[128,512]{1,0:T(8,128)(2,1)}, u32[]{:S(2)}) copy-start(bf16[128,512]{1,0:T(8,128)(2,1)} %gather_fusion.9) | copy-start | bytes 393220
  54.1 7.4 %copy-start.9 = (bf16[2,256,128]{2,1,0:T(8,128)(2,1)S(1)}, bf16[2,256,128]{2,1,0:T(8,128)(2,1)}, u32[]{:S(2)}) copy-start(bf16[2,256,128]{2,1,0:T(8,128)(2,1)} %copy-done.7) | copy-start | bytes 393220
  54.1 12.1 %copy-start.5 = (f32[768,512]{1,0:T(8,128)S(1)}, f32[768,512]{1,0:T(8,128)}, u32[]{:S(2)}) copy-start(f32[768,512]{1,0:T(8,128)} %get-tuple-element.102) | copy-start | bytes 4718596
  55.0 11.2 %copy-start.2 = (f32[768,512]{1,0:T(8,128)S(1)}, f32[768,512]{1,0:T(8,128)}, u32[]{:S(2)}) copy-start(f32[768,512]{1,0:T(8,128)} %param.24) | copy-start | bytes 4718596
  55.1 6.4 %collective-permute-start.4 = (bf16[128,512]{1,0:T(8,128)(2,1)S(1)}, bf16[128,512]{1,0:T(8,128)(2,1)S(1)}, u32[]{:S(2)}, u32[]{:S(2)}) collective-permute-start(bf16[128,512]{1,0:T(8,128)(2,1)S(1)} %broadcast_select_fusion.5), channel_id=1, source_target_pairs={{0,2},{2,4},{4,6},{6,8},{8,10},{10,12},{12,14},{14,16},{16,18},{18... | collective-permute-start | bytes 393224 | tf_op jit(solution)/shard_map/ppermute | solution.py:16
  59.1 6.9 %collective-permute-start.5 = (bf16[128,512]{1,0:T(8,128)(2,1)S(1)}, bf16[128,512]{1,0:T(8,128)(2,1)S(1)}, u32[]{:S(2)}, u32[]{:S(2)}) collective-permute-start(bf16[128,512]{1,0:T(8,128)(2,1)S(1)} %broadcast_select_fusion.1), channel_id=1, source_target_pairs={{2,0},{4,2},{6,4},{8,6},{10,8},{12,10},{14,12},{16,14},{18,16},{20... | collective-permute-start | bytes 393224 | tf_op jit(solution)/shard_map/ppermute | solution.py:16
  66.2 2.0 %copy-start.3 = (f32[3,256,512]{2,1,0:T(8,128)}, f32[3,256,512]{2,1,0:T(8,128)S(1)}, u32[]{:S(2)}) copy-start(f32[3,256,512]{2,1,0:T(8,128)S(1)} %fusion.16) | copy-start | bytes 4718596
  72.6 0.9 copy-start.12
  72.6 6.6 %copy-start.11 = (bf16[128,512]{1,0:T(8,128)(2,1)S(1)}, bf16[128,512]{1,0:T(8,128)(2,1)}, u32[]{:S(2)}) copy-start(bf16[128,512]{1,0:T(8,128)(2,1)} %gather_fusion.11) | copy-start | bytes 393220
  72.6 9.1 %copy-start.10 = (bf16[2,256,128]{2,1,0:T(8,128)(2,1)S(1)}, bf16[2,256,128]{2,1,0:T(8,128)(2,1)}, u32[]{:S(2)}) copy-start(bf16[2,256,128]{2,1,0:T(8,128)(2,1)} %copy-done.7) | copy-start | bytes 393220
  72.6 13.7 %copy-start.6 = (f32[768,512]{1,0:T(8,128)S(1)}, f32[768,512]{1,0:T(8,128)}, u32[]{:S(2)}) copy-start(f32[768,512]{1,0:T(8,128)} %get-tuple-element.102) | copy-start | bytes 4718596
  73.5 12.9 %copy-start.4 = (f32[3,256,512]{2,1,0:T(8,128)S(1)}, f32[3,256,512]{2,1,0:T(8,128)}, u32[]{:S(2)}) copy-start(f32[3,256,512]{2,1,0:T(8,128)} %copy-done.3) | copy-start | bytes 4718596
  73.6 8.1 %collective-permute-start.6 = (bf16[128,512]{1,0:T(8,128)(2,1)S(1)}, bf16[128,512]{1,0:T(8,128)(2,1)S(1)}, u32[]{:S(2)}, u32[]{:S(2)}) collective-permute-start(bf16[128,512]{1,0:T(8,128)(2,1)S(1)} %broadcast_select_fusion.4), channel_id=1, source_target_pairs={{0,2},{2,4},{4,6},{6,8},{8,10},{10,12},{12,14},{14,16},{16,18},{18... | collective-permute-start | bytes 393224 | tf_op jit(solution)/shard_map/ppermute | solution.py:16
  79.3 6.9 %collective-permute-start.7 = (bf16[128,512]{1,0:T(8,128)(2,1)S(1)}, bf16[128,512]{1,0:T(8,128)(2,1)S(1)}, u32[]{:S(2)}, u32[]{:S(2)}) collective-permute-start(bf16[128,512]{1,0:T(8,128)(2,1)S(1)} %broadcast_select_fusion), channel_id=1, source_target_pairs={{2,0},{4,2},{6,4},{8,6},{10,8},{12,10},{14,12},{16,14},{18,16},{20... | collective-permute-start | bytes 393224 | tf_op jit(solution)/shard_map/ppermute | solution.py:16
  86.4 0.7 copy-start.21
where the time goes:
time: 127 us
  blocking collectives  45.5 us (36%)
  starting transfers between devices  24.8 us (20%)
  local copies, waits for them, and re-layouts  18.5 us (15%)
  waiting for transfers between devices  17.1 us (13%)
  matrix products  10.2 us (8%)
  other arithmetic  9.43 us (7%)
    psum x1, blocking collectives, local(): res_total = lax.psum(res_part, 'space')  39.1 us
    ppermute x8, starting transfers between devices, passed_along(): return lax.ppermute(x, axis, pairs)  24.8 us
    ppermute x8, waiting for transfers between devices, passed_along(): return lax.ppermute(x, axis, pairs)  17.1 us
    convert_element_type x4, other arithmetic, apply_operator(): flat_rounded = direction.astype(jnp.bfloat16)  6.41 us
    gather x4, local copies, waits for them, and re-layouts, apply_operator(): send_down = jnp.take(flat_rounded, boundary[0], axis=0)  5.69 us
    gather x4, local copies, waits for them, and re-layouts, apply_operator(): send_up = jnp.take(flat_rounded, boundary[1], axis=0)  5.35 us
    dot_general x4, matrix products, apply_operator(): jnp.einsum('akij,akjs->ais', couple_full, beside, preferred_element_type=...  5.08 us
    gather x4, local copies, waits for them, and re-layouts, apply_operator(): beside = rounded[neighbours]  4.97 us
  transfers between devices with their start and end apart: 8, of which 6 were waited for; matrix products, arithmetic and copies ran while one was open for 4% of the time, Pallas kernels for 0%

commit v1 on v0

v1 whole, which is shorter than its diff:
```python
import functools

import jax
import jax.numpy as jnp
from jax import lax
from jax.experimental import pallas as pl
from jax.experimental.pallas import tpu as pltpu
from jax.sharding import PartitionSpec as P

SWEEPS = 4
CHUNKS = 2
MESH = pl.DeviceIdType.MESH

centre = 4.0
half_width = 2.0


def sweep_weights():
    sigma = centre / half_width
    ratio = 1.0 / sigma
    weights = []
    for _ in range(SWEEPS - 1):
        ratio_new = 1.0 / (2.0 * sigma - ratio)
        weights.append((ratio_new * ratio, 2.0 * ratio_new / half_width))
        ratio = ratio_new
    return weights


def kernel(
    n_space, n_src,
    rhs_ref, diag_ref, couple_ref, halo_ref, nbr_ref, bnd_ref,
    total, misfit_ref,
    res, dirn, rounded, weights, gmat, picks, bounds, outbox, inbox, red_b, red_r,
    rhs_sem, bnd_sem, own_sem, op_send, op_recv, halo_send, halo_recv, sums_send, sums_recv,
):
    me = lax.axis_index("space")
    core = lax.axis_index("src")
    aggs, size, depth = weights.shape
    edges, width = res.shape
    nbrs = couple_ref.shape[1]
    halo = bnd_ref.shape[1]
    part = size // n_src
    cols = width // CHUNKS

    def span(c):
        return pl.ds(c * cols, cols)

    rhs_loads = [
        pltpu.make_async_copy(rhs_ref.at[:, span(c)], res.at[:, span(c)], rhs_sem.at[c])
        for c in range(CHUNKS)
    ]
    bnd_load = pltpu.make_async_copy(bnd_ref, bounds, bnd_sem)
    bnd_load.start()
    for load in rhs_loads:
        load.start()
    rows = pl.ds(pl.multiple_of(core * part, part), part)
    pieces = [(diag_ref, weights.at[:, rows, pl.ds(0, size)])]
    for k in range(nbrs):
        pieces.append((couple_ref.at[:, k], weights.at[:, rows, pl.ds((k + 1) * size, size)]))
    pieces.append((halo_ref, gmat.at[:, rows]))
    own = [pltpu.make_async_copy(a, b, own_sem.at[i]) for i, (a, b) in enumerate(pieces)]
    for load in own:
        load.start()

    barrier = pltpu.get_barrier_semaphore()

    def greet_space(k, carry):
        pl.semaphore_signal(
            barrier, inc=1, device_id={"space": lax.rem(me + k, n_space)}, device_id_type=MESH
        )
        return carry

    lax.fori_loop(1, n_space, greet_space, 0)
    for k in range(1, n_src):
        pl.semaphore_signal(
            barrier, inc=1, device_id={"src": lax.rem(core + k, n_src)}, device_id_type=MESH
        )

    bnd_load.wait()
    at = lax.broadcasted_iota(jnp.int32, (edges, halo), 0)
    for i, side in enumerate((1, 0)):
        hit = (at == bounds[side : side + 1, :]).astype(jnp.float32)
        picks[pl.ds(i * halo, halo), :] = hit.T.astype(jnp.bfloat16)

    @pl.when(me == 0)
    def _():
        inbox[:, :, 0] = jnp.zeros_like(inbox[:, :, 0])

    @pl.when(me == n_space - 1)
    def _():
        inbox[:, :, 1] = jnp.zeros_like(inbox[:, :, 1])

    def pack(s, c):
        picked = jnp.dot(picks[...], rounded[:, :, span(c)].reshape(edges, cols), preferred_element_type=jnp.float32)
        outbox[s, c] = picked.astype(jnp.bfloat16).reshape(2, halo, cols)

    def passed(s, c, side):
        to = lax.rem(me + 1, n_space) if side == 0 else lax.rem(me + n_space - 1, n_space)
        return pltpu.make_async_remote_copy(
            src_ref=outbox.at[s, c, side],
            dst_ref=inbox.at[s, c, side],
            send_sem=halo_send.at[s, c, side],
            recv_sem=halo_recv.at[s, c, side],
            device_id={"space": to},
            device_id_type=MESH,
        )

    sends = (me < n_space - 1, me > 0)
    takes = (me > 0, me < n_space - 1)

    def send(s, c):
        for side in range(2):
            pl.when(sends[side])(passed(s, c, side).start)

    def take(s, c):
        for side in range(2):
            pl.when(takes[side])(passed(s, c, side).wait_recv)

    def share(buffer, index):
        def one(k, carry):
            pltpu.make_async_remote_copy(
                src_ref=buffer.at[me],
                dst_ref=buffer.at[me],
                send_sem=sums_send.at[index],
                recv_sem=sums_recv.at[index],
                device_id={"space": lax.rem(me + k, n_space)},
                device_id_type=MESH,
            ).start()
            return carry

        lax.fori_loop(1, n_space, one, 0)

    def collected(buffer, sem):
        others = buffer.at[pl.ds(0, n_space - 1)]
        pltpu.make_async_copy(others, others, sem).wait()

    for c in range(CHUNKS):
        rhs_loads[c].wait()
        right = res[:, span(c)]
        start = right / centre
        dirn[:, span(c)] = start
        rounded[:, :, span(c)] = start.astype(jnp.bfloat16).reshape(aggs, size, cols)
        pack(0, c)
        if c == 0:
            pl.semaphore_wait(barrier, n_space - 1 + n_src - 1)
        send(0, c)
        red_b[me, :, span(c)] = jnp.sum(right * right, axis=0, keepdims=True)

    moves = []
    for k in range(1, n_src):
        for i, (a, b) in enumerate(pieces):
            move = pltpu.make_async_remote_copy(
                src_ref=a,
                dst_ref=b,
                send_sem=op_send.at[k - 1, i],
                recv_sem=op_recv.at[k - 1, i],
                device_id={"src": lax.rem(core + k, n_src)},
                device_id_type=MESH,
            )
            move.start()
            moves.append(move)
    share(red_b, 0)
    for load in own:
        load.wait()
    for move in moves:
        move.wait()

    def local_part(c):
        for a in range(aggs):
            group = pl.ds(a * size, size)
            beside = [rounded[a, :, span(c)]]
            for k in range(nbrs):
                beside.append(rounded[nbr_ref[k, a], :, span(c)])
            res[group, span(c)] -= jnp.dot(
                weights[a], jnp.concatenate(beside, axis=0), preferred_element_type=jnp.float32
            )

    def halo_part(s, c):
        for side, a in ((0, 0), (1, aggs - 1)):
            group = pl.ds(a * size, size)
            res[group, span(c)] -= jnp.dot(
                gmat[side], inbox[s, c, side], preferred_element_type=jnp.float32
            )

    for c in range(CHUNKS):
        local_part(c)

    steps = sweep_weights()
    for s in range(SWEEPS - 1):
        keep, gain = steps[s]
        for c in range(CHUNKS):
            take(s, c)
            halo_part(s, c)
            before = dirn[:, span(c)]
            after = keep * before + gain * res[:, span(c)]
            rounded[:, :, span(c)] = after.astype(jnp.bfloat16).reshape(aggs, size, cols)
            pack(s + 1, c)
            send(s + 1, c)
            dirn[:, span(c)] = after
            if s == 0:
                total[:, span(c)] = before + after
            else:
                total[:, span(c)] += after
            local_part(c)

    for c in range(CHUNKS):
        take(SWEEPS - 1, c)
        halo_part(SWEEPS - 1, c)
        left = res[:, span(c)]
        red_r[me, :, span(c)] = jnp.sum(left * left, axis=0, keepdims=True)
    share(red_r, 1)
    collected(red_b, sums_recv.at[0])
    bb = jnp.sum(red_b[...], axis=0)
    for s in range(SWEEPS):
        for c in range(CHUNKS):
            for side in range(2):
                pl.when(sends[side])(passed(s, c, side).wait_send)
    collected(red_b, sums_send.at[0])
    collected(red_r, sums_recv.at[1])
    rr = jnp.sum(red_r[...], axis=0)
    misfit_ref[...] = jnp.sqrt(rr / (bb + 1e-06))
    collected(red_r, sums_send.at[1])


def local(n_space, n_src, rhs, diag_blocks, couple_blocks, halo_weight, neighbours, boundary):
    edges, width = rhs.shape
    aggs, part, size = diag_blocks.shape
    nbrs = couple_blocks.shape[1]
    halo = boundary.shape[1]
    cols = width // CHUNKS
    bf16, f32 = jnp.bfloat16, jnp.float32
    dma = pltpu.SemaphoreType.DMA
    outside = pl.BlockSpec(memory_space=pltpu.HBM)
    inside = pl.BlockSpec(memory_space=pltpu.VMEM)
    result, misfit = pl.pallas_call(
        functools.partial(kernel, n_space, n_src),
        out_shape=(
            jax.ShapeDtypeStruct((edges, width), f32),
            jax.ShapeDtypeStruct((1, width), f32),
        ),
        in_specs=[outside] * 4 + [pl.BlockSpec(memory_space=pltpu.SMEM), outside],
        out_specs=(inside, inside),
        scratch_shapes=[
            pltpu.VMEM((edges, width), f32),
            pltpu.VMEM((edges, width), f32),
            pltpu.VMEM((aggs, size, width), bf16),
            pltpu.VMEM((aggs, size, (nbrs + 1) * size), bf16),
            pltpu.VMEM((2, size, halo), bf16),
            pltpu.VMEM((2 * halo, edges), bf16),
            pltpu.VMEM((2, halo), jnp.int32),
            pltpu.VMEM((SWEEPS, CHUNKS, 2, halo, cols), bf16),
            pltpu.VMEM((SWEEPS, CHUNKS, 2, halo, cols), bf16),
            pltpu.VMEM((n_space, 1, width), f32),
            pltpu.VMEM((n_space, 1, width), f32),
            dma((CHUNKS,)),
            dma,
            dma((nbrs + 2,)),
            dma((max(n_src - 1, 1), nbrs + 2)),
            dma((max(n_src - 1, 1), nbrs + 2)),
            dma((SWEEPS, CHUNKS, 2)),
            dma((SWEEPS, CHUNKS, 2)),
            dma((2,)),
            dma((2,)),
        ],
        compiler_params=pltpu.CompilerParams(
            collective_id=0, has_side_effects=True, vmem_limit_bytes=48 * 1024 * 1024
        ),
    )(rhs, diag_blocks, couple_blocks, halo_weight, neighbours.T, boundary)
    return result, misfit.reshape(width)


def solution(mesh):
    placed = (
        P("space", "src"),
        P("space", "src", None),
        P("space", None, "src", None),
        P("space", "src", None),
        P("space", None),
        P("space", None),
    )
    body = functools.partial(local, mesh.shape["space"], mesh.shape["src"])
    return jax.shard_map(
        body, mesh=mesh, in_specs=placed, out_specs=(P("space", "src"), P("src")), check_vma=False
    )
```

time: 127 us -> 45.7 us (0.36)
  blocking collectives: 45.5 us -> 0 us
  Pallas kernels: 0 us -> 37.5 us
  starting transfers between devices: 24.8 us -> 0 us
  waiting for transfers between devices: 17.1 us -> 0 us
  local copies, waits for them, and re-layouts: 18.5 us -> 7.24 us
  matrix products: 10.2 us -> 0 us
  other arithmetic: 9.43 us -> 0 us
    psum x1 -> x0, blocking collectives: 39.1 us -> none  [local(): res_total = lax.psum(res_part, 'space')]
    pallas_call x0 -> x1, Pallas kernels: none -> 37.5 us  [local(): pl.pallas_call(functools.partial(kernel, n_space, n_src), out_shape=(jax....]
    ppermute x8 -> x0, starting transfers between devices: 24.8 us -> none  [passed_along(): return lax.ppermute(x, axis, pairs)]
    ppermute x8 -> x0, waiting for transfers between devices: 17.1 us -> none  [passed_along(): return lax.ppermute(x, axis, pairs)]
    gather x12 -> x0, local copies, waits for them, and re-layouts: 16 us -> none  [the longest x4 5.69 us: apply_operator(): send_down = jnp.take(flat_rounded, boundary[0], axis=0)]
    dot_general x16 -> x0, matrix products: 10.2 us -> none  [the longest x4 5.08 us: apply_operator(): jnp.einsum('akij,akjs->ais', couple_full, beside, preferred_element_type=...]
    all_gather x3 -> x0, blocking collectives: 6.47 us -> none  [the longest x1 2.37 us: local(): lax.all_gather(couple_blocks, 'src', axis=2, tiled=True)]
    convert_element_type x4 -> x0, other arithmetic: 6.41 us -> none  [apply_operator(): flat_rounded = direction.astype(jnp.bfloat16)]
  transfers between devices with their start and end apart: 8 -> 0, of which waited for: 6 -> 0; matrix products, arithmetic and copies ran while one was open for 4% -> 0% of each run, Pallas kernels for 0% -> 0%
where the time goes in v1:
time: 45.7 us; the launch traced here: 45.4 us
  Pallas kernels  37.5 us (82%)
  local copies, waits for them, and re-layouts  7.24 us (16%)
  between operations  0.65 us (1%)
    pallas_call x1, Pallas kernels, local(): pl.pallas_call(functools.partial(kernel, n_space, n_src), out_shape=(jax....  37.5 us
    unnamed x14, local copies, waits for them, and re-layouts  7.24 us

profile of v1, /device:TPU:0, one launch (start us, length us, event | category | flops | bytes accessed | tf_op | source)
XLA Modules:
  0.0 45.4 jit_solution(6668927303879425049)
XLA Ops:
  0.6 0.0 copy-start
  0.6 1.4 %copy-done = f32[768,512]{1,0:T(8,128)S(1)} copy-done((f32[768,512]{1,0:T(8,128)S(1)}, f32[768,512]{1,0:T(8,128)}, u32[]{:S(2)}) %copy-start) | copy-done | bytes 1572888
  2.0 0.0 copy-start.1
  2.0 1.0 %copy-done.1 = bf16[3,2,128,256]{3,2,1,0:T(8,128)(2,1)S(1)} copy-done((bf16[3,2,128,256]{3,2,1,0:T(8,128)(2,1)S(1)}, bf16[3,2,128,256]{3,2,1,0:T(8,128)(2,1)}, u32[]{:S(2)}) %copy-start.1) | copy-done | bytes 393240
  3.0 0.0 copy-start.2
  3.0 0.9 %copy-done.2 = bf16[3,128,256]{2,1,0:T(8,128)(2,1)S(1)} copy-done((bf16[3,128,256]{2,1,0:T(8,128)(2,1)S(1)}, bf16[3,128,256]{2,1,0:T(8,128)(2,1)}, u32[]{:S(2)}) %copy-start.2) | copy-done | bytes 196632
  4.0 0.0 copy-start.3
  4.0 0.8 %copy-done.3 = bf16[2,128,128]{2,1,0:T(8,128)(2,1)S(1)} copy-done((bf16[2,128,128]{2,1,0:T(8,128)(2,1)S(1)}, bf16[2,128,128]{2,1,0:T(8,128)(2,1)}, u32[]{:S(2)}) %copy-start.3) | copy-done | bytes 65560
  4.8 0.0 copy-start.4
  4.8 0.7 %copy-done.4 = s32[3,2]{0,1:T(2,128)S(1)} copy-done((s32[3,2]{0,1:T(2,128)S(1)}, s32[3,2]{0,1:T(2,128)}, u32[]{:S(2)}) %copy-start.4) | copy-done | bytes 48
  5.5 0.0 copy-start.5
  5.5 0.7 %copy-done.5 = s32[2,128]{1,0:T(2,128)S(1)} copy-done((s32[2,128]{1,0:T(2,128)S(1)}, s32[2,128]{1,0:T(2,128)}, u32[]{:S(2)}) %copy-start.5) | copy-done | bytes 1048
  6.2 37.5 %shard_map.77 = (f32[768,512]{1,0:T(8,128)S(1)}, f32[1,512]{1,0:T(1,128)S(1)}) custom-call(f32[768,512]{1,0:T(8,128)S(1)} %copy-done, bf16[3,128,256]{2,1,0:T(8,128)(2,1)S(1)} %copy-done.2, bf16[3,2,128,256]{3,2,1,0:T(8,128)(2,1)S(1)} %copy-done.1, bf16[2,128,128]{2,1,0:T(8,128)(2,1)S(1)} %copy-done.3, s32[2,3]{1,0:T(2,128)S(1)} %bitcast.3, ...), custom_call_target="tpu_custom_call" | custom-call | tf_op jit(solution)/shard_map/pallas_call | solution.py:235
  43.6 1.1 %copy.10 = f32[768,512]{1,0:T(8,128)} copy(f32[768,512]{1,0:T(8,128)S(1)} %get-tuple-element.8) | data formatting | bytes 3145728
  44.8 0.6 %copy.11 = f32[512]{0:T(512)} copy(f32[512]{0:T(512)S(1)} %bitcast.2) | data formatting | bytes 4096
Async XLA Ops:
  0.6 1.4 %copy-start = (f32[768,512]{1,0:T(8,128)S(1)}, f32[768,512]{1,0:T(8,128)}, u32[]{:S(2)}) copy-start(f32[768,512]{1,0:T(8,128)} %rhs_ref.1) | copy-start | bytes 4718596
  2.0 1.0 %copy-start.1 = (bf16[3,2,128,256]{3,2,1,0:T(8,128)(2,1)S(1)}, bf16[3,2,128,256]{3,2,1,0:T(8,128)(2,1)}, u32[]{:S(2)}) copy-start(bf16[3,2,128,256]{3,2,1,0:T(8,128)(2,1)} %couple_ref.1) | copy-start | bytes 1179652
  3.0 0.9 %copy-start.2 = (bf16[3,128,256]{2,1,0:T(8,128)(2,1)S(1)}, bf16[3,128,256]{2,1,0:T(8,128)(2,1)}, u32[]{:S(2)}) copy-start(bf16[3,128,256]{2,1,0:T(8,128)(2,1)} %diag_ref.1) | copy-start | bytes 589828
  4.0 0.8 %copy-start.3 = (bf16[2,128,128]{2,1,0:T(8,128)(2,1)S(1)}, bf16[2,128,128]{2,1,0:T(8,128)(2,1)}, u32[]{:S(2)}) copy-start(bf16[2,128,128]{2,1,0:T(8,128)(2,1)} %halo_ref.1) | copy-start | bytes 196612
  4.8 0.7 %copy-start.4 = (s32[3,2]{0,1:T(2,128)S(1)}, s32[3,2]{0,1:T(2,128)}, u32[]{:S(2)}) copy-start(s32[3,2]{0,1:T(2,128)} %param.10) | copy-start | bytes 76
  5.5 0.7 %copy-start.5 = (s32[2,128]{1,0:T(2,128)S(1)}, s32[2,128]{1,0:T(2,128)}, u32[]{:S(2)}) copy-start(s32[2,128]{1,0:T(2,128)} %bnd_ref.1) | copy-start | bytes 3076

commit v2 on v1

--- a/solution.py
+++ b/solution.py
@@ -8,7 +8,8 @@
 from jax.sharding import PartitionSpec as P
 
 SWEEPS = 4
-CHUNKS = 2
+CHUNKS = 4
+GROUP = 2
 MESH = pl.DeviceIdType.MESH
 
 centre = 4.0
@@ -29,9 +30,9 @@
 def kernel(
     n_space, n_src,
     rhs_ref, diag_ref, couple_ref, halo_ref, nbr_ref, bnd_ref,
-    total, misfit_ref,
-    res, dirn, rounded, weights, gmat, picks, bounds, outbox, inbox, red_b, red_r,
-    rhs_sem, bnd_sem, own_sem, op_send, op_recv, halo_send, halo_recv, sums_send, sums_recv,
+    sol_ref, misfit_ref,
+    res, dirn, rounded, total, weights, gmat, picks, bounds, outbox, inbox, red_b, red_r,
+    rhs_sem, bnd_sem, out_sem, own_sem, op_send, op_recv, halo_send, halo_recv, sums_send, sums_recv, heard,
 ):
     me = lax.axis_index("space")
     core = lax.axis_index("src")
@@ -42,8 +43,8 @@
     part = size // n_src
     cols = width // CHUNKS
 
-    def span(c):
-        return pl.ds(c * cols, cols)
+    def span(c, many=1):
+        return pl.ds(c * cols, many * cols)
 
     rhs_loads = [
         pltpu.make_async_copy(rhs_ref.at[:, span(c)], res.at[:, span(c)], rhs_sem.at[c])
@@ -64,17 +65,39 @@
 
     barrier = pltpu.get_barrier_semaphore()
 
-    def greet_space(k, carry):
+    def greet(axis, to):
+        pl.semaphore_signal(barrier, inc=1, device_id={axis: to}, device_id_type=MESH)
+
+    def across(j):
+        return me + (1 - 2 * (lax.div(me, 1 << j) % 2)) * (1 << j)
+
+    rounds = []
+    if n_space & (n_space - 1) == 0:
+        dims = n_space.bit_length() - 1
+        for j in range(dims):
+            greet("space", across(j))
+        pl.when(me > 0)(lambda: greet("space", me - 1))
+        pl.when(me < n_space - 1)(lambda: greet("space", me + 1))
+        greeted = dims + (me > 0).astype(jnp.int32) + (me < n_space - 1).astype(jnp.int32)
+        rounds = list(range(1, dims))
+    else:
+
+        @pl.loop(1, n_space)
+        def _(k):
+            greet("space", lax.rem(me + k, n_space))
+
+        greeted = n_space - 1
+    for k in range(1, n_src):
+        greet("src", lax.rem(core + k, n_src))
+
+    def hear(j):
+        if j > 1:
+            pl.semaphore_wait(heard.at[j - 1], 1)
         pl.semaphore_signal(
-            barrier, inc=1, device_id={"space": lax.rem(me + k, n_space)}, device_id_type=MESH
+            heard.at[j], inc=1, device_id={"space": across(j)}, device_id_type=MESH
         )
-        return carry
-
-    lax.fori_loop(1, n_space, greet_space, 0)
-    for k in range(1, n_src):
-        pl.semaphore_signal(
-            barrier, inc=1, device_id={"src": lax.rem(core + k, n_src)}, device_id_type=MESH
-        )
+
+    last_round = rounds[-1] if rounds else None
 
     bnd_load.wait()
     at = lax.broadcasted_iota(jnp.int32, (edges, halo), 0)
@@ -142,7 +165,7 @@
         rounded[:, :, span(c)] = start.astype(jnp.bfloat16).reshape(aggs, size, cols)
         pack(0, c)
         if c == 0:
-            pl.semaphore_wait(barrier, n_space - 1 + n_src - 1)
+            pl.semaphore_wait(barrier, greeted + n_src - 1)
         send(0, c)
         red_b[me, :, span(c)] = jnp.sum(right * right, axis=0, keepdims=True)
 
@@ -159,19 +182,21 @@
             )
             move.start()
             moves.append(move)
-    share(red_b, 0)
+    if rounds:
+        hear(rounds.pop(0))
     for load in own:
         load.wait()
     for move in moves:
         move.wait()
 
     def local_part(c):
+        wide = span(c, GROUP)
         for a in range(aggs):
             group = pl.ds(a * size, size)
-            beside = [rounded[a, :, span(c)]]
+            beside = [rounded[a, :, wide]]
             for k in range(nbrs):
-                beside.append(rounded[nbr_ref[k, a], :, span(c)])
-            res[group, span(c)] -= jnp.dot(
+                beside.append(rounded[nbr_ref[k, a], :, wide])
+            res[group, wide] -= jnp.dot(
                 weights[a], jnp.concatenate(beside, axis=0), preferred_element_type=jnp.float32
             )
 
@@ -182,9 +207,10 @@
                 gmat[side], inbox[s, c, side], preferred_element_type=jnp.float32
             )
 
-    for c in range(CHUNKS):
+    for c in range(0, CHUNKS, GROUP):
         local_part(c)
 
+    stores = []
     steps = sweep_weights()
     for s in range(SWEEPS - 1):
         keep, gain = steps[s]
@@ -201,8 +227,21 @@
                 total[:, span(c)] = before + after
             else:
                 total[:, span(c)] += after
-            local_part(c)
-
+            if s == SWEEPS - 2:
+                store = pltpu.make_async_copy(
+                    total.at[:, span(c)], sol_ref.at[:, span(c)], out_sem.at[c]
+                )
+                store.start()
+                stores.append(store)
+            if (c + 1) % GROUP == 0:
+                local_part(c + 1 - GROUP)
+                if rounds:
+                    hear(rounds.pop(0))
+
+    assert not rounds
+    if last_round is not None:
+        pl.semaphore_wait(heard.at[last_round], 1)
+    share(red_b, 0)
     for c in range(CHUNKS):
         take(SWEEPS - 1, c)
         halo_part(SWEEPS - 1, c)
@@ -211,6 +250,8 @@
     share(red_r, 1)
     collected(red_b, sums_recv.at[0])
     bb = jnp.sum(red_b[...], axis=0)
+    for store in stores:
+        store.wait()
     for s in range(SWEEPS):
         for c in range(CHUNKS):
             for side in range(2):
@@ -239,11 +280,12 @@
             jax.ShapeDtypeStruct((1, width), f32),
         ),
         in_specs=[outside] * 4 + [pl.BlockSpec(memory_space=pltpu.SMEM), outside],
-        out_specs=(inside, inside),
+        out_specs=(outside, inside),
         scratch_shapes=[
             pltpu.VMEM((edges, width), f32),
             pltpu.VMEM((edges, width), f32),
             pltpu.VMEM((aggs, size, width), bf16),
+            pltpu.VMEM((edges, width), f32),
             pltpu.VMEM((aggs, size, (nbrs + 1) * size), bf16),
             pltpu.VMEM((2, size, halo), bf16),
             pltpu.VMEM((2 * halo, edges), bf16),
@@ -254,6 +296,7 @@
             pltpu.VMEM((n_space, 1, width), f32),
             dma((CHUNKS,)),
             dma,
+            dma((CHUNKS,)),
             dma((nbrs + 2,)),
             dma((max(n_src - 1, 1), nbrs + 2)),
             dma((max(n_src - 1, 1), nbrs + 2)),
@@ -261,9 +304,10 @@
             dma((SWEEPS, CHUNKS, 2)),
             dma((2,)),
             dma((2,)),
+            pltpu.SemaphoreType.REGULAR((max(n_space.bit_length() - 1, 1),)),
         ],
         compiler_params=pltpu.CompilerParams(
-            collective_id=0, has_side_effects=True, vmem_limit_bytes=48 * 1024 * 1024
+            collective_id=0, has_side_effects=True, vmem_limit_bytes=67043328
         ),
     )(rhs, diag_blocks, couple_blocks, halo_weight, neighbours.T, boundary)
     return result, misfit.reshape(width)

time: 45.7 us -> 41.7 us (0.912)
  local copies, waits for them, and re-layouts: 7.24 us -> 3.25 us
    unnamed x14 -> x4, local copies, waits for them, and re-layouts: 7.24 us -> 3.25 us
where the time goes in v2:
time: 41.7 us; the launch traced here: 41.5 us
  Pallas kernels  37.6 us (90%)
  local copies, waits for them, and re-layouts  3.25 us (8%)
  between operations  0.65 us (2%)
    pallas_call x1, Pallas kernels, local(): pl.pallas_call(functools.partial(kernel, n_space, n_src), out_shape=(jax....  37.6 us
    unnamed x4, local copies, waits for them, and re-layouts  3.25 us

profile of v2, /device:TPU:0, one launch (start us, length us, event | category | flops | bytes accessed | tf_op | source)
XLA Modules:
  0.0 41.5 jit_solution(1815189292138367312)
XLA Ops:
  0.6 37.6 %shard_map.77 = (f32[768,512]{1,0:T(8,128)}, f32[1,512]{1,0:T(1,128)}) custom-call(f32[768,512]{1,0:T(8,128)} %rhs_ref.1, bf16[3,128,256]{2,1,0:T(8,128)(2,1)} %diag_ref.1, bf16[3,2,128,256]{3,2,1,0:T(8,128)(2,1)} %couple_ref.1, bf16[2,128,128]{2,1,0:T(8,128)(2,1)} %halo_ref.1, s32[2,3]{1,0:T(2,128)} %bitcast.3, s32[2,128]{1,0:T(2,128)} %bnd_ref.1), custom_call_target="tpu_custom_call" | custom-call | tf_op jit(solution)/shard_map/pallas_call | solution.py:276
  38.2 0.0 copy-start
  38.2 2.7 %copy.10 = f32[768,512]{1,0:T(8,128)} copy(f32[768,512]{1,0:T(8,128)} %get-tuple-element.8) | data formatting | bytes 3145728
  40.9 0.0 copy-done
  40.9 0.6 %copy.11 = f32[512]{0:T(512)} copy(f32[512]{0:T(512)S(1)} %bitcast.2) | data formatting | bytes 4096
Async XLA Ops:
  38.2 2.7 %copy-start = (f32[1,512]{1,0:T(1,128)S(1)}, f32[1,512]{1,0:T(1,128)}, u32[]{:S(2)}) copy-start(f32[1,512]{1,0:T(1,128)} %get-tuple-element.5) | copy-start | bytes 6148

commit v3 on v2

--- a/solution.py
+++ b/solution.py
@@ -9,7 +9,7 @@
 
 SWEEPS = 4
 CHUNKS = 4
-GROUP = 2
+GROUP = 1
 MESH = pl.DeviceIdType.MESH
 
 centre = 4.0
@@ -30,9 +30,9 @@
 def kernel(
     n_space, n_src,
     rhs_ref, diag_ref, couple_ref, halo_ref, nbr_ref, bnd_ref,
-    sol_ref, misfit_ref,
-    res, dirn, rounded, total, weights, gmat, picks, bounds, outbox, inbox, red_b, red_r,
-    rhs_sem, bnd_sem, out_sem, own_sem, op_send, op_recv, halo_send, halo_recv, sums_send, sums_recv, heard,
+    total, misfit_ref,
+    res, dirn, rounded, weights, gmat, picks, bounds, outbox, inbox, red_b, red_r,
+    rhs_sem, bnd_sem, own_sem, op_send, op_recv, halo_send, halo_recv, sums_send, sums_recv, heard,
 ):
     me = lax.axis_index("space")
     core = lax.axis_index("src")
@@ -210,7 +210,6 @@
     for c in range(0, CHUNKS, GROUP):
         local_part(c)
 
-    stores = []
     steps = sweep_weights()
     for s in range(SWEEPS - 1):
         keep, gain = steps[s]
@@ -227,12 +226,6 @@
                 total[:, span(c)] = before + after
             else:
                 total[:, span(c)] += after
-            if s == SWEEPS - 2:
-                store = pltpu.make_async_copy(
-                    total.at[:, span(c)], sol_ref.at[:, span(c)], out_sem.at[c]
-                )
-                store.start()
-                stores.append(store)
             if (c + 1) % GROUP == 0:
                 local_part(c + 1 - GROUP)
                 if rounds:
@@ -250,8 +243,6 @@
     share(red_r, 1)
     collected(red_b, sums_recv.at[0])
     bb = jnp.sum(red_b[...], axis=0)
-    for store in stores:
-        store.wait()
     for s in range(SWEEPS):
         for c in range(CHUNKS):
             for side in range(2):
@@ -276,16 +267,15 @@
     result, misfit = pl.pallas_call(
         functools.partial(kernel, n_space, n_src),
         out_shape=(
-            jax.ShapeDtypeStruct((edges, width), f32),
+            pltpu.VMEM((edges, width), f32),
             jax.ShapeDtypeStruct((1, width), f32),
         ),
         in_specs=[outside] * 4 + [pl.BlockSpec(memory_space=pltpu.SMEM), outside],
-        out_specs=(outside, inside),
+        out_specs=(pl.BlockSpec(memory_space=pltpu.VMEM), inside),
         scratch_shapes=[
             pltpu.VMEM((edges, width), f32),
             pltpu.VMEM((edges, width), f32),
             pltpu.VMEM((aggs, size, width), bf16),
-            pltpu.VMEM((edges, width), f32),
             pltpu.VMEM((aggs, size, (nbrs + 1) * size), bf16),
             pltpu.VMEM((2, size, halo), bf16),
             pltpu.VMEM((2 * halo, edges), bf16),
@@ -296,7 +286,6 @@
             pltpu.VMEM((n_space, 1, width), f32),
             dma((CHUNKS,)),
             dma,
-            dma((CHUNKS,)),
             dma((nbrs + 2,)),
             dma((max(n_src - 1, 1), nbrs + 2)),
             dma((max(n_src - 1, 1), nbrs + 2)),
@@ -307,7 +296,7 @@
             pltpu.SemaphoreType.REGULAR((max(n_space.bit_length() - 1, 1),)),
         ],
         compiler_params=pltpu.CompilerParams(
-            collective_id=0, has_side_effects=True, vmem_limit_bytes=67043328
+            collective_id=0, has_side_effects=True, vmem_limit_bytes=67043328 - edges * width * 4
         ),
     )(rhs, diag_blocks, couple_blocks, halo_weight, neighbours.T, boundary)
     return result, misfit.reshape(width)

time: 41.7 us -> 39.8 us (0.954)
  local copies, waits for them, and re-layouts: 3.25 us -> 1.73 us
    unnamed x4, local copies, waits for them, and re-layouts: 3.25 us -> 1.73 us
where the time goes in v3:
time: 39.8 us; the launch traced here: 39.6 us
  Pallas kernels  37.2 us (93%)
  local copies, waits for them, and re-layouts  1.73 us (4%)
  between operations  0.65 us (2%)
    pallas_call x1, Pallas kernels, local(): pl.pallas_call(functools.partial(kernel, n_space, n_src), out_shape=(pltp...  37.2 us
    unnamed x4, local copies, waits for them, and re-layouts  1.73 us

profile of v3, /device:TPU:0, one launch (start us, length us, event | category | flops | bytes accessed | tf_op | source)
XLA Modules:
  0.0 39.6 jit_solution(5651221745549484238)
XLA Ops:
  0.6 37.2 %shard_map.77 = (f32[768,512]{1,0:T(8,128)S(1)}, f32[1,512]{1,0:T(1,128)}) custom-call(f32[768,512]{1,0:T(8,128)} %rhs_ref.1, bf16[3,128,256]{2,1,0:T(8,128)(2,1)} %diag_ref.1, bf16[3,2,128,256]{3,2,1,0:T(8,128)(2,1)} %couple_ref.1, bf16[2,128,128]{2,1,0:T(8,128)(2,1)} %halo_ref.1, s32[2,3]{1,0:T(2,128)} %bitcast.3, s32[2,128]{1,0:T(2,128)} %bnd_ref.1), custom_call_target="tpu_custom_call" | custom-call | tf_op jit(solution)/shard_map/pallas_call | solution.py:267
  37.9 0.0 copy-start
  37.9 1.1 %copy.10 = f32[768,512]{1,0:T(8,128)} copy(f32[768,512]{1,0:T(8,128)S(1)} %get-tuple-element.6) | data formatting | bytes 3145728
  39.0 0.0 copy-done
  39.0 0.6 %copy.11 = f32[512]{0:T(512)} copy(f32[512]{0:T(512)S(1)} %bitcast.2) | data formatting | bytes 4096
Async XLA Ops:
  37.9 1.2 %copy-start = (f32[1,512]{1,0:T(1,128)S(1)}, f32[1,512]{1,0:T(1,128)}, u32[]{:S(2)}) copy-start(f32[1,512]{1,0:T(1,128)} %get-tuple-element.5) | copy-start | bytes 6148
